TPU v7x, 128 devices: a whole 4x4x4 slice. The times are simulated.
128 devices in a mesh: src: 16 (over x, z_lo, core), freq: 8 (over y, z_hi).
Axes of the slice: x: 4, y: 4, z: 4 (z_hi: 2, z_lo: 2; z = z_hi * 2 + z_lo), core: 2. Of those that a mesh axis runs over, the one named last changes fastest.
Arguments:
- receivers: bfloat16 [8, 16, 2, 256, 512], P('freq', 'src'), may hold values from -6 to 6
- data: bfloat16 [8, 2, 8192, 2048], P('freq', None, None, 'src'), may hold values from -0.046875 to 0.046875
- block_of_slot: int32 [16], replicated, may hold values from 0 to 15, each once
- receiver_order: int32 [256], replicated, may hold values from 0 to 255, each once
Outputs:
- traces: bfloat16 [256, 2048, 256], P('freq', 'src')
Inputs may be any that keep to these rules, and one draw needn't show every extreme that they name: `block_of_slot`: each of the 16 bounce blocks is held in exactly one slot. `receiver_order`: each receiver appears in exactly one trace row.
All inputs are finite; a program needn't handle non-finite values.
Results may differ from a plain program's by a relative error of at most 0.0049.
Values may be sent and summed in bfloat16 or wider, within the bound.
A program may use at most 64 MiB of HBM per device.

v0:
```python
import math
import jax
import jax.numpy as jnp
import numpy as np
from jax import lax
from jax.sharding import PartitionSpec as P

NT = 256


def tables(count):
    times = np.arange(NT)
    bins = (2 * np.arange(count) + 1) * (NT // (4 * count))
    angle = bins[:, None] * times[None, :] % NT * (2.0 * math.pi / NT)
    full = np.stack([np.cos(angle), -np.sin(angle)], 1) * count ** (-0.5)
    return full.astype(np.float32)


def body(receivers, data, block_of_slot, receiver_order):
    width = receivers.shape[4]
    blocks = lax.all_gather(receivers[0], "src", axis=0, tiled=True)
    slots = blocks.shape[0]
    rows = data[0].reshape(2, slots, width, data.shape[3])
    slot_of_block = jnp.argsort(block_of_slot)
    moved = jnp.take(blocks, slot_of_block, axis=0)
    acc = jnp.einsum("jcrk,djks->cdrs", moved, rows, preferred_element_type=jnp.float32)
    spectra = jnp.stack([acc[0, 0] - acc[1, 1], acc[0, 1] + acc[1, 0]], 0).astype(jnp.bfloat16)
    ordered = jnp.take(spectra, receiver_order, axis=1)[None]
    got = lax.all_to_all(ordered, "freq", split_axis=2, concat_axis=0, tiled=True)
    table = jnp.asarray(tables(got.shape[0]))
    high = table.astype(jnp.bfloat16)
    low = (table - high.astype(jnp.float32)).astype(jnp.bfloat16)
    value = jnp.einsum("fcrs,fct->rst", got, high, preferred_element_type=jnp.float32)
    value = value + jnp.einsum("fcrs,fct->rst", got, low, preferred_element_type=jnp.float32)
    return value.astype(jnp.bfloat16)


def solution(mesh):
    placed = (P("freq", "src", None, None, None), P("freq", None, None, "src"), P(), P())
    return jax.shard_map(
        body, mesh=mesh, in_specs=placed, out_specs=P("freq", "src", None), check_vma=False
    )
```

profile of v0, /device:TPU:0, one launch (start us, length us, event | category | flops | bytes accessed | tf_op | source)
XLA Modules:
  0.0 104.4 jit_solution(16391787386407409647)
XLA Ops:
  6.5 0.0 all-gather.3.cloned.1.call-start
  6.5 0.7 all-gather.3.cloned.1.call-update
  7.3 1.9 %sort.17 = (s32[16]{0:T(128)}, s32[16]{0:T(128)S(1)}) sort(s32[16]{0:T(128)} %param.7, s32[16]{0:T(128)S(1)} %iota.4), dimensions={0}, to_apply=%region_0.0 | sort | flops 64 | bytes 256 | tf_op jit(solution)/shard_map/jit(argsort)/sort | solution.py:24
  9.2 0.7 compare_select_fusion
  9.9 0.7 compare_and_fusion.1
  10.6 53.1 %all-gather.3.cloned.1.call-done = bf16[16,1,2,256,512]{4,3,2,1,0:T(8,128)(2,1)} async-done(((bf16[1,1,2,256,512]{4,3,2,1,0:T(8,128)(2,1)}), bf16[16,1,2,256,512]{4,3,2,1,0:T(8,128)(2,1)}) %all-gather.3.cloned.1.call-update) | async-done | bytes 8388624 | tf_op jit(solution)/shard_map/all_gather | solution.py:21
  63.7 8.1 %gather_fusion = bf16[16,2,256,512]{3,2,1,0:T(8,128)(2,1)} fusion(bf16[16,2,256,512]{3,2,1,0:T(8,128)(2,1)} %bitcast.46, s32[1024]{0:T(1024)S(1)} %pad_clamp_fusion.1), kind=kCustom, calls=%fused_computation | custom fusion | bytes 16777280 | tf_op jit(solution)/shard_map/jit(_take)/gather | solution.py:25
  71.8 0.0 copy-start
  71.8 0.0 copy-start.1
  71.8 7.0 %fusion.3 = f32[2,2,256,128]{3,2,1,0:T(8,128)S(1)} fusion(bf16[2,16,512,128,1]{3,2,1,0,4:T(8,128)(2,1)} %bitcast.49, bf16[16,2,256,512]{3,2,1,0:T(8,128)(2,1)} %gather_fusion, pred[16]{0:T(512)(128)(4,1)S(1)} %compare_and_fusion), kind=kOutput, calls=%fused_computation.7 | convolution fusion | flops 2151677952 | bytes 13107216 | tf_op jit(solution)/shard_map/jcrk,djks->cdrs/dot_general | solution.py:26
  78.8 0.1 copy.15
  79.0 0.9 gather_fusion.1
  79.9 0.3 fusion.11
  80.3 14.4 %all_to_all.18 = bf16[1,2,256,128]{3,1,0,2:T(2,128)(2,1)S(1)} all-to-all(bf16[1,2,256,128]{3,1,0,2:T(2,128)(2,1)S(1)} %fusion.11), channel_id=1, replica_groups=mesh['src'=16,'freq'=8] {'freq'}, dimensions={2} | all-to-all | bytes 262144 | tf_op jit(solution)/shard_map/all_to_all | solution.py:29
  94.7 0.0 copy-done
  94.7 0.8 fusion.9
  95.5 0.0 copy-done.1
  95.5 2.1 %fusion.2 = bf16[32,128,256]{2,1,0:T(8,128)(2,1)} fusion(f32[32,128,256,1]{2,1,3,0:T(8,128)S(1)} %fusion.9, bf16[8,2,256,1]{2,0,1,3:T(8,128)(2,1)S(1)} %copy-done.1, bf16[1,2,8,32,128]{4,1,3,2,0:T(2,128)(2,1)S(1)} %bitcast.48), kind=kOutput, calls=%fused_computation.6 | convolution fusion | flops 35651584 | bytes 6430720 | tf_op jit(solution)/shard_map/fcrs,fct->rst/dot_general | solution.py:34
  (7 shorter events, 0.1 us)
Async XLA Ops:
  6.5 57.1 %all-gather.3.cloned.1.call-start = ((), (), s32[]{:S(2)}) async-start(), calls=%async_computation.1 | async-start | bytes 8912896 | tf_op jit(solution)/shard_map/all_gather | solution.py:21
  71.8 22.9 %copy-start = (bf16[8,2,256,1]{2,0,1,3:T(8,128)(2,1)S(1)}, bf16[8,2,256,1]{2,0,1,3:T(8,128)(2,1)}, u32[]{:S(2)}) copy-start(bf16[8,2,256,1]{2,0,1,3:T(8,128)(2,1)} %constant.39) | copy-start | bytes 24580
  71.8 23.7 %copy-start.1 = (bf16[8,2,256,1]{2,0,1,3:T(8,128)(2,1)S(1)}, bf16[8,2,256,1]{2,0,1,3:T(8,128)(2,1)}, u32[]{:S(2)}) copy-start(bf16[8,2,256,1]{2,0,1,3:T(8,128)(2,1)} %constant.40) | copy-start | bytes 24580
Sparse Core Ops, SparseCore 0:
  9.0 54.5 all-gather.2
where the time goes:
time: 105 us; the launch traced here: 104 us
  waiting for transfers between devices  53.8 us (51%)
  blocking collectives  14.4 us (14%)
  between operations  13.5 us (13%)
  matrix products  9.82 us (9%)
  local copies, waits for them, and re-layouts  9.21 us (9%)
  other arithmetic  3.68 us (4%)
    all_gather x1, waiting for transfers between devices, body(): blocks = lax.all_gather(receivers[0], 'src', axis=0, tiled=True)  53.1 us
    all_to_all x1, blocking collectives, body(): lax.all_to_all(ordered, 'freq', split_axis=2, concat_axis=0, tiled=True)  14.4 us
    gather x1, local copies, waits for them, and re-layouts, body(): moved = jnp.take(blocks, slot_of_block, axis=0)  8.13 us
    dot_general x1, matrix products, body(): jnp.einsum('jcrk,djks->cdrs', moved, rows, preferred_element_type=jnp.flo...  6.97 us
  transfers between devices with their start and end apart: 1, of which 1 were waited for; matrix products, arithmetic and copies ran while one was open for 3% of the time, Pallas kernels for 0%

commit v1 on v0

--- a/solution.py
+++ b/solution.py
@@ -18,7 +18,9 @@
 
 def body(receivers, data, block_of_slot, receiver_order):
     width = receivers.shape[4]
-    blocks = lax.all_gather(receivers[0], "src", axis=0, tiled=True)
+    block = receivers[0]
+    stack = jnp.stack([block] * lax.axis_size("src"))
+    blocks = jnp.concatenate(lax.all_to_all(stack, "src", 0, 0), axis=0)
     slots = blocks.shape[0]
     rows = data[0].reshape(2, slots, width, data.shape[3])
     slot_of_block = jnp.argsort(block_of_slot)

time: 105 us -> 178 us (1.70)
  waiting for transfers between devices: 53.8 us -> 131 us
  between operations: 13.5 us -> 0.12 us
  starting transfers between devices: 0.01 us -> 6.05 us
  local copies, waits for them, and re-layouts: 9.21 us -> 14.4 us
  other arithmetic: 3.68 us -> 1.67 us
    all_to_all x0 -> x1, waiting for transfers between devices: none -> 131 us  [body(): blocks = jnp.concatenate(lax.all_to_all(stack, 'src', 0, 0), axis=0)]
    all_gather x1 -> x0, waiting for transfers between devices: 53.1 us -> none  [body(): blocks = lax.all_gather(receivers[0], 'src', axis=0, tiled=True)]
    all_to_all x0 -> x1, starting transfers between devices: none -> 6.05 us  [body(): blocks = jnp.concatenate(lax.all_to_all(stack, 'src', 0, 0), axis=0)]
    another operation x0 -> x1, local copies, waits for them, and re-layouts: none -> 5.2 us  [body(): stack = jnp.stack([block] * lax.axis_size('src'))]
  transfers between devices with their start and end apart: 1 -> 1, of which waited for: 1 -> 1; matrix products, arithmetic and copies ran while one was open for 3% -> 1% of each run, Pallas kernels for 0% -> 0%
where the time goes in v1:
time: 178 us
  waiting for transfers between devices  131 us (74%)
  blocking collectives  15.2 us (9%)
  local copies, waits for them, and re-layouts  14.4 us (8%)
  matrix products  9.82 us (6%)
  starting transfers between devices  6.05 us (3%)
    all_to_all x1, waiting for transfers between devices, body(): blocks = jnp.concatenate(lax.all_to_all(stack, 'src', 0, 0), axis=0)  131 us
    all_to_all x1, blocking collectives, body(): lax.all_to_all(ordered, 'freq', split_axis=2, concat_axis=0, tiled=True)  15.2 us
    gather x1, local copies, waits for them, and re-layouts, body(): moved = jnp.take(blocks, slot_of_block, axis=0)  8.13 us
    dot_general x1, matrix products, body(): jnp.einsum('jcrk,djks->cdrs', moved, rows, preferred_element_type=jnp.flo...  6.97 us
    all_to_all x1, starting transfers between devices, body(): blocks = jnp.concatenate(lax.all_to_all(stack, 'src', 0, 0), axis=0)  6.05 us
    another operation x1, local copies, waits for them, and re-layouts, body(): stack = jnp.stack([block] * lax.axis_size('src'))  5.2 us
  transfers between devices with their start and end apart: 1, of which 1 were waited for; matrix products, arithmetic and copies ran while one was open for 1% of the time, Pallas kernels for 0%

profile of v1, /device:TPU:0, one launch (start us, length us, event | category | flops | bytes accessed | tf_op | source)
XLA Modules:
  0.0 177.9 jit_solution(1676271520003362899)
XLA Ops:
  0.0 5.2 %stack.9 = bf16[16,1,2,256,512]{4,3,2,1,0:T(8,128)(2,1)} broadcast(bf16[2,256,512]{2,1,0:T(8,128)(2,1)} %bitcast.49), dimensions={2,3,4} | broadcast | bytes 8912896 | tf_op jit(solution)/shard_map/stack | solution.py:22
  5.2 0.0 copy-start.3
  5.2 0.0 copy-start.2
  5.2 6.1 %all-to-all-start = ((bf16[16,1,2,256,512]{4,3,2,1,0:T(8,128)(2,1)}), bf16[16,1,2,256,512]{4,3,2,1,0:T(8,128)(2,1)}, u32[]{:S(2)}, u32[]{:S(2)}) async-start(bf16[16,1,2,256,512]{4,3,2,1,0:T(8,128)(2,1)} %stack.9), calls=%async_computation | async-start | bytes 16777216 | tf_op jit(solution)/shard_map/all_to_all | solution.py:23
  11.3 0.0 copy-done.3
  11.3 1.2 sort.17
  12.5 0.0 copy-done.2
  12.6 130.6 %all-to-all-done = bf16[16,1,2,256,512]{4,3,2,1,0:T(8,128)(2,1)} async-done(((bf16[16,1,2,256,512]{4,3,2,1,0:T(8,128)(2,1)}), bf16[16,1,2,256,512]{4,3,2,1,0:T(8,128)(2,1)}, u32[]{:S(2)}, u32[]{:S(2)}) %all-to-all-start) | async-done | bytes 8388640 | tf_op jit(solution)/shard_map/all_to_all | solution.py:23
  143.2 8.1 %gather_fusion = bf16[16,2,256,512]{3,2,1,0:T(8,128)(2,1)} fusion(bf16[16,2,256,512]{3,2,1,0:T(8,128)(2,1)} %bitcast.1, s32[1024]{0:T(1024)S(1)} %pad_clamp_fusion.1), kind=kCustom, calls=%fused_computation | custom fusion | bytes 16777280 | tf_op jit(solution)/shard_map/jit(_take)/gather | solution.py:27
  151.4 0.0 copy-start
  151.4 0.0 copy-start.1
  151.4 7.0 %fusion.3 = f32[2,2,256,128]{3,2,1,0:T(8,128)S(1)} fusion(bf16[2,16,512,128,1]{3,2,1,0,4:T(8,128)(2,1)} %bitcast.50, bf16[16,2,256,512]{3,2,1,0:T(8,128)(2,1)} %gather_fusion, pred[16]{0:T(512)(128)(4,1)S(1)} %compare_and_fusion), kind=kOutput, calls=%fused_computation.7 | convolution fusion | flops 2151677952 | bytes 13107216 | tf_op jit(solution)/shard_map/jcrk,djks->cdrs/dot_general | solution.py:28
  158.4 0.1 copy.14
  158.6 0.9 gather_fusion.1
  159.5 0.3 fusion.11
  159.8 15.2 %all_to_all.23 = bf16[1,2,256,128]{3,1,0,2:T(2,128)(2,1)S(1)} all-to-all(bf16[1,2,256,128]{3,1,0,2:T(2,128)(2,1)S(1)} %fusion.11), channel_id=1, replica_groups=mesh['src'=16,'freq'=8] {'freq'}, dimensions={2} | all-to-all | bytes 262144 | tf_op jit(solution)/shard_map/all_to_all | solution.py:31
  175.0 0.0 copy-done
  175.0 0.8 fusion.9
  175.8 0.0 copy-done.1
  175.8 2.1 %fusion.2 = bf16[32,128,256]{2,1,0:T(8,128)(2,1)} fusion(f32[32,128,256,1]{2,1,3,0:T(8,128)S(1)} %fusion.9, bf16[8,2,256,1]{2,0,1,3:T(8,128)(2,1)S(1)} %copy-done.1, bf16[1,2,8,32,128]{4,1,3,2,0:T(2,128)(2,1)S(1)} %bitcast.48), kind=kOutput, calls=%fused_computation.6 | convolution fusion | flops 35651584 | bytes 6430720 | tf_op jit(solution)/shard_map/fcrs,fct->rst/dot_general | solution.py:36
  (9 shorter events, 0.1 us)
Async XLA Ops:
  5.2 6.1 %copy-start.3 = (s32[16]{0:T(128)S(1)}, s32[16]{0:T(128)}, u32[]{:S(2)}) copy-start(s32[16]{0:T(128)} %param.7) | copy-start | bytes 196
  5.2 7.3 %copy-start.2 = (s32[256]{0:T(256)S(1)}, s32[256]{0:T(256)}, u32[]{:S(2)}) copy-start(s32[256]{0:T(256)} %param.8) | copy-start | bytes 3076
  5.2 138.0 %all-to-all-start = ((bf16[16,1,2,256,512]{4,3,2,1,0:T(8,128)(2,1)}), bf16[16,1,2,256,512]{4,3,2,1,0:T(8,128)(2,1)}, u32[]{:S(2)}, u32[]{:S(2)}) async-start(bf16[16,1,2,256,512]{4,3,2,1,0:T(8,128)(2,1)} %stack.9), calls=%async_computation | async-start | bytes 16777216 | tf_op jit(solution)/shard_map/all_to_all | solution.py:23
  151.4 23.7 %copy-start = (bf16[8,2,256,1]{2,0,1,3:T(8,128)(2,1)S(1)}, bf16[8,2,256,1]{2,0,1,3:T(8,128)(2,1)}, u32[]{:S(2)}) copy-start(bf16[8,2,256,1]{2,0,1,3:T(8,128)(2,1)} %constant.39) | copy-start | bytes 24580
  151.4 24.4 %copy-start.1 = (bf16[8,2,256,1]{2,0,1,3:T(8,128)(2,1)S(1)}, bf16[8,2,256,1]{2,0,1,3:T(8,128)(2,1)}, u32[]{:S(2)}) copy-start(bf16[8,2,256,1]{2,0,1,3:T(8,128)(2,1)} %constant.40) | copy-start | bytes 24580
